TPU v7x, 512 devices: a whole 4x8x8 slice. The times are simulated.
512 devices in a mesh: dp: 64 (over x, y, core), tensor: 8 (over z).
Axes of the slice: x: 4, y: 8, z: 8, core: 2. Of those that a mesh axis runs over, the one named last changes fastest.
Arguments:
- features: bfloat16 [65536, 4096], P(('dp', 'tensor')), may hold values from -20 to 20
- key_grads: bfloat16 [65536, 1024], P('dp', 'tensor'), may hold values from -20 to 20
- error_in: bfloat16 [64, 4096, 1024], P('dp', None, 'tensor'), may hold values from -24 to 24
- selected: int32 [64, 8, 128], P('dp', 'tensor'), may hold values from 0 to 4095, as said below
- bin_edges: int32 [17], replicated, may hold values from 0 to 4096, as said below
- threshold: int32 [1], replicated, may hold values from 1 to 15
- moment: float32 [4096, 1024], P('dp', 'tensor'), may hold values from -2 to 2
- second: float32 [4096, 1024], P('dp', 'tensor'), may hold values from 0.05 to 2
- master: float32 [4096, 1024], P('dp', 'tensor'), may hold values from -0.0625 to 0.0625
Outputs:
- keys: bfloat16 [65536, 1024], P('dp', 'tensor')
- error_out: bfloat16 [64, 4096, 1024], P('dp', None, 'tensor')
- moment_new: float32 [4096, 1024], P('dp', 'tensor')
- second_new: float32 [4096, 1024], P('dp', 'tensor')
- master_new: float32 [4096, 1024], P('dp', 'tensor')
Inputs may be any that keep to these rules, and one draw needn't show every extreme that they name: Each device's 128 rows are distinct; the rows o * 64 to (o + 1) * 64 - 1 form owner o's region, and one device's row of selected names at most 6 rows of one region; there is one region, the same for every row of selected, that receives exactly 6 blocks from each row; every other region receives at most 6 from a row. bin_edges[0] = 0, bin_edges[16] = 4096, strictly increasing.
All inputs are finite; a program needn't handle non-finite values.
Results may differ from a plain program's by a relative error of at most 0.001.
The roundings to bfloat16 on the way count: a program that leaves them out, or rounds other values in their place, can miss the bound.
Values may be sent and summed in bfloat16 or wider, within the bound.
A program may use at most 64 MiB of HBM per device.

v0:
```python
import math

import jax
import jax.numpy as jnp
from jax import lax
from jax.sharding import PartitionSpec as P

CAP = 6


beta_first = 0.9
beta_second = 0.95
learn_rate = 0.001
decay_rate = 0.1
epsilon = 1e-06
adam_epsilon = 1e-08
step_count = 10.0


def copy_for_each(value, axis):
    devices = lax.axis_size(axis)
    return lax.all_to_all(
        jnp.broadcast_to(value[None], (devices, *value.shape)), axis, 0, 0, tiled=True
    )


def over_copies(value, axis):
    everything = copy_for_each(value, axis)
    return jnp.sum(everything, axis=0)


def in_one_piece(arrays, axis, split_dim, concat_dim, along):
    widths = [math.prod(a.shape[along:]) for a in arrays]
    both = jnp.concatenate(
        [a.reshape(*a.shape[:along], w) for a, w in zip(arrays, widths)], axis=along
    )
    filled = lax.all_to_all(both, axis, split_axis=split_dim, concat_axis=concat_dim, tiled=True)
    blocks = jnp.split(filled, [sum(widths[:k]) for k in range(1, len(widths))], axis=along)
    return tuple(
        (b.reshape(*filled.shape[:along], *a.shape[along:]) for a, b in zip(arrays, blocks))
    )


def in_order(blocks, dim):
    dims = list(blocks.shape[1:])
    dims[dim] *= blocks.shape[0]
    return jnp.moveaxis(blocks, 0, dim).reshape(dims)


def gather_directly(value, axis, dim):
    return in_order(copy_for_each(value, axis), dim)


def shards(features, key_grads, error_in, selected, bin_edges, threshold, moment, second, master):
    highest = lax.Precision.HIGHEST
    whole = lax.all_gather(features, "tensor", axis=0, tiled=True)
    summed = lax.dot_general(
        whole, key_grads, (((0,), (0,)), ((), ())), preferred_element_type=jnp.float32
    )
    summed = summed + error_in[0].astype(jnp.float32)
    row_total = summed.shape[0]
    width_head = summed.shape[1]
    owners = lax.axis_size("dp")
    region = row_total // owners
    squares = jnp.sum(summed * summed, axis=1)
    row_ids = lax.iota(jnp.int32, row_total)
    member = (
        (row_ids[:, None] >= bin_edges[None, :-1]) & (row_ids[:, None] < bin_edges[None, 1:])
    ).astype(jnp.float32)
    energy = over_copies(jnp.dot(squares, member, precision=highest), "dp")
    widths = (bin_edges[1:] - bin_edges[:-1]).astype(jnp.float32)
    levels = lax.iota(jnp.int32, widths.shape[0])
    normal = 1.0 / jnp.sqrt(energy / (owners * width_head * widths) + epsilon)
    scale = jnp.where(levels >= threshold[0], normal, jnp.ones_like(normal))
    row_scale = jnp.dot(member, scale, precision=highest)
    chosen_ids = selected[0, 0]
    chosen = jnp.zeros((row_total,), jnp.float32).at[chosen_ids].set(1.0)
    kept = summed * chosen[:, None]
    error_out = (summed - kept).astype(jnp.bfloat16)[None]
    scaled = kept * row_scale[:, None]
    owner_of = chosen_ids // region
    owner_hot = (owner_of[:, None] == lax.iota(jnp.int32, owners)[None, :]).astype(jnp.int32)
    earlier = jnp.cumsum(owner_hot, axis=0) - owner_hot
    rank = jnp.sum(earlier * owner_hot, axis=1)
    slot = owner_of * CAP + rank
    outgoing = jnp.zeros((owners * CAP, width_head), jnp.float32).at[slot].set(scaled[chosen_ids])
    offsets = (
        jnp.full((owners * CAP,), region, jnp.float32)
        .at[slot]
        .set((chosen_ids % region).astype(jnp.float32))
    )
    arrived, places = in_one_piece(
        (outgoing.reshape(owners, CAP, width_head), offsets.reshape(owners, CAP)), "dp", 0, 0, 2
    )
    place_hot = (places.reshape(-1)[:, None] == lax.iota(jnp.float32, region)[None, :]).astype(
        jnp.float32
    )
    grad = lax.dot_general(
        place_hot, arrived.reshape(-1, width_head), (((0,), (0,)), ((), ())), precision=highest
    )
    moment_new = beta_first * moment + (1.0 - beta_first) * grad
    second_new = beta_second * second + (1.0 - beta_second) * grad * grad
    first_hat = moment_new / (1.0 - beta_first**step_count)
    second_hat = second_new / (1.0 - beta_second**step_count)
    master_new = master - learn_rate * (
        first_hat / (jnp.sqrt(second_hat) + adam_epsilon) + decay_rate * master
    )
    weight = master_new.astype(jnp.bfloat16)
    keys = jnp.dot(whole, gather_directly(weight, "dp", 0), preferred_element_type=jnp.float32)
    return (keys.astype(jnp.bfloat16), error_out, moment_new, second_new, master_new)


def solution(mesh):
    in_specs = (
        P(("dp", "tensor"), None),
        P("dp", "tensor"),
        P("dp", None, "tensor"),
        P("dp", "tensor", None),
        P(),
        P(),
        P("dp", "tensor"),
        P("dp", "tensor"),
        P("dp", "tensor"),
    )
    out_specs = (
        P("dp", "tensor"),
        P("dp", None, "tensor"),
        P("dp", "tensor"),
        P("dp", "tensor"),
        P("dp", "tensor"),
    )
    return jax.shard_map(shards, mesh=mesh, in_specs=in_specs, out_specs=out_specs, check_vma=False)
```

profile of v0, /device:TPU:1, one launch (start us, length us, event | category | flops | bytes accessed | tf_op | source)
XLA Modules:
  0.0 216.0 jit_solution(11072930889191832977)
XLA Ops:
  7.2 0.0 copy-start
  7.2 0.0 copy-start.5
  7.2 0.0 copy-start.4
  7.2 0.0 all-gather.2.cloned.1.call-start
  7.2 0.7 all-gather.2.cloned.1.call-update
  7.9 1.5 copy.28
  9.4 0.0 copy-done.5
  9.5 0.1 fusion.15
  9.5 0.2 reduce_window_sum.11
  9.7 0.2 select_reduce_fusion
  9.9 0.0 copy-done.4
  9.9 0.1 fusion.41
  10.0 103.0 %all-gather.2.cloned.1.call-done = bf16[1024,4096]{1,0:T(8,128)(2,1)} async-done(((bf16[128,4096]{1,0:T(8,128)(2,1)}), bf16[1024,4096]{1,0:T(8,128)(2,1)}) %all-gather.2.cloned.1.call-update) | async-done | bytes 8388624 | tf_op jit(solution)/shard_map/all_gather | solution.py:56
  112.9 0.0 copy-done
  112.9 4.9 %multiply_reduce_fusion = (f32[4096]{0:T(1024)S(1)}, f32[4096,128]{0,1:T(8,128)S(1)}) fusion(bf16[1,4096,128]{1,2,0:T(8,128)(2,1)S(1)} %copy.28, bf16[1024,4096]{1,0:T(8,128)(2,1)} %all-gather.2.cloned.1.call-done, bf16[1024,128]{1,0:T(8,128)(2,1)S(1)} %copy-done), kind=kOutput, calls=%fused_computation.8 | convolution fusion | flops 1075834880 | bytes 11812864 | tf_op jit(solution)/shard_map/dot_general | solution.py:57
  117.8 0.3 convolution_bitcast_fusion
  118.2 0.7 broadcast_in_dim.17
  118.8 10.5 %all-to-all-start = ((f32[64,1,16]{2,1,0:T(1,128)}), f32[64,1,16]{2,1,0:T(1,128)S(1)}, u32[]{:S(2)}, u32[]{:S(2)}) async-start(f32[64,1,16]{2,1,0:T(1,128)} %broadcast_in_dim.17), calls=%async_computation | async-start | bytes 65536 | tf_op jit(solution)/shard_map/all_to_all | solution.py:22
  130.1 1.0 scatter_custom_fusion.2
  131.0 0.9 reshape_reshape.4
  132.0 1.0 scatter_custom_fusion
  133.0 5.7 %all-to-all-done = f32[64,1,16]{2,1,0:T(1,128)S(1)} async-done(((f32[64,1,16]{2,1,0:T(1,128)}), f32[64,1,16]{2,1,0:T(1,128)S(1)}, u32[]{:S(2)}, u32[]{:S(2)}) %all-to-all-start) | async-done | bytes 4128 | tf_op jit(solution)/shard_map/all_to_all | solution.py:22
  138.6 0.1 reduce_sum.32
  138.7 0.3 fusion.4
  139.0 1.7 fusion.2
  140.8 1.9 copy.30
  142.7 1.9 scatter_custom_fusion.1
  144.6 1.0 reshape.153
  145.5 1.0 pad_maximum_fusion
  146.5 0.0 copy-start.1
  146.5 0.0 copy-start.2
  146.6 0.0 copy-start.3
  146.6 0.5 reshape.204
  147.0 15.6 %all_to_all.16 = f32[64,1,774]{2,1,0:T(1,128)S(1)} all-to-all(f32[64,1,774]{2,1,0:T(1,128)S(1)} %reshape.204), channel_id=1, replica_groups=mesh['dp'=64,'tensor'=8] {'dp'}, dimensions={0} | all-to-all | bytes 396288 | tf_op jit(solution)/shard_map/all_to_all | solution.py:37
  162.6 0.5 broadcast.187
  163.1 1.2 reduce.3
  164.3 0.3 reshape.205
  164.6 0.1 slice_reduce_fusion
  164.8 0.1 eq.33
  164.9 0.0 copy-done.1
  164.9 0.0 copy-done.2
  164.9 0.0 copy-done.3
  164.9 1.1 fusion.39
  166.0 1.3 broadcast_in_dim.19
  167.3 6.2 %all-to-all-start.2 = ((bf16[64,64,128]{2,1,0:T(8,128)(2,1)}), bf16[64,64,128]{2,1,0:T(8,128)(2,1)S(1)}, u32[]{:S(2)}, u32[]{:S(2)}) async-start(bf16[64,64,128]{2,1,0:T(8,128)(2,1)} %broadcast_in_dim.19), calls=%async_computation.2 | async-start | bytes 2097152 | tf_op jit(solution)/shard_map/all_to_all | solution.py:22
  173.5 1.3 copy.33
  174.8 27.2 %all-to-all-done.2 = bf16[64,64,128]{2,1,0:T(8,128)(2,1)S(1)} async-done(((bf16[64,64,128]{2,1,0:T(8,128)(2,1)}), bf16[64,64,128]{2,1,0:T(8,128)(2,1)S(1)}, u32[]{:S(2)}, u32[]{:S(2)}) %all-to-all-start.2) | async-done | bytes 1048608 | tf_op jit(solution)/shard_map/all_to_all | solution.py:22
  202.0 6.3 %fusion.1 = bf16[1024,128]{0,1:T(8,128)(2,1)S(1)} fusion(bf16[4096,128]{1,0:T(8,128)(2,1)S(1)} %bitcast.57, bf16[1024,4096]{1,0:T(8,128)(2,1)} %all-gather.2.cloned.1.call-done), kind=kOutput, calls=%fused_computation.10 | convolution fusion | flops 1073872896 | bytes 9699328 | tf_op jit(solution)/shard_map/dot_general | solution.py:109
  208.3 0.8 copy.32
  (6 shorter events, 0.1 us)
Async XLA Ops:
  7.2 105.8 %copy-start = (bf16[1024,128]{1,0:T(8,128)(2,1)S(1)}, bf16[1024,128]{1,0:T(8,128)(2,1)}, u32[]{:S(2)}) copy-start(bf16[1024,128]{1,0:T(8,128)(2,1)} %param.10) | copy-start | bytes 786436
  7.2 2.2 %copy-start.5 = (s32[1,1,128]{2,1,0:T(1,128)S(1)}, s32[1,1,128]{2,1,0:T(1,128)}, u32[]{:S(2)}) copy-start(s32[1,1,128]{2,1,0:T(1,128)} %param.12) | copy-start | bytes 1540
  7.2 2.7 %copy-start.4 = (s32[17]{0:T(128)S(1)}, s32[17]{0:T(128)}, u32[]{:S(2)}) copy-start(s32[17]{0:T(128)} %param.13) | copy-start | bytes 208
  7.2 105.7 %all-gather.2.cloned.1.call-start = ((), (), s32[]{:S(2)}) async-start(), calls=%async_computation.3 | async-start | bytes 9437184 | tf_op jit(solution)/shard_map/all_gather | solution.py:56
  118.8 19.8 %all-to-all-start = ((f32[64,1,16]{2,1,0:T(1,128)}), f32[64,1,16]{2,1,0:T(1,128)S(1)}, u32[]{:S(2)}, u32[]{:S(2)}) async-start(f32[64,1,16]{2,1,0:T(1,128)} %broadcast_in_dim.17), calls=%async_computation | async-start | bytes 65536 | tf_op jit(solution)/shard_map/all_to_all | solution.py:22
  146.5 18.4 %copy-start.1 = (f32[64,128]{1,0:T(8,128)S(1)}, f32[64,128]{1,0:T(8,128)}, u32[]{:S(2)}) copy-start(f32[64,128]{1,0:T(8,128)} %param.17) | copy-start | bytes 98308
  146.5 18.4 %copy-start.2 = (f32[64,128]{1,0:T(8,128)S(1)}, f32[64,128]{1,0:T(8,128)}, u32[]{:S(2)}) copy-start(f32[64,128]{1,0:T(8,128)} %param.15) | copy-start | bytes 98308
  146.6 18.4 %copy-start.3 = (f32[64,128]{1,0:T(8,128)S(1)}, f32[64,128]{1,0:T(8,128)}, u32[]{:S(2)}) copy-start(f32[64,128]{1,0:T(8,128)} %param.16) | copy-start | bytes 98308
  167.3 34.7 %all-to-all-start.2 = ((bf16[64,64,128]{2,1,0:T(8,128)(2,1)}), bf16[64,64,128]{2,1,0:T(8,128)(2,1)S(1)}, u32[]{:S(2)}, u32[]{:S(2)}) async-start(bf16[64,64,128]{2,1,0:T(8,128)(2,1)} %broadcast_in_dim.19), calls=%async_computation.2 | async-start | bytes 2097152 | tf_op jit(solution)/shard_map/all_to_all | solution.py:22
Sparse Core Ops, SparseCore 0:
  10.1 102.8 all-gather.1
where the time goes:
time: 217 us; the launch traced here: 216 us
  waiting for transfers between devices  137 us (63%)
  starting transfers between devices  16.8 us (8%)
  blocking collectives  15.6 us (7%)
  local copies, waits for them, and re-layouts  14.9 us (7%)
  between operations  14.9 us (7%)
  matrix products  12.8 us (6%)
  other arithmetic  4.47 us (2%)
    all_gather x1, waiting for transfers between devices, shards(): whole = lax.all_gather(features, 'tensor', axis=0, tiled=True)  103 us
    all_to_all x2, waiting for transfers between devices, copy_for_each(): lax.all_to_all(jnp.broadcast_to(value[None], (devices, *value.shape)), ax...  32.9 us
    all_to_all x2, starting transfers between devices, copy_for_each(): lax.all_to_all(jnp.broadcast_to(value[None], (devices, *value.shape)), ax...  16.7 us
    all_to_all x1, blocking collectives, in_one_piece(): lax.all_to_all(both, axis, split_axis=split_dim, concat_axis=concat_dim,...  15.6 us
    dot_general x1, matrix products, shards(): jnp.dot(whole, gather_directly(weight, 'dp', 0), preferred_element_type=j...  6.29 us
    dot_general x1, matrix products, shards(): lax.dot_general(whole, key_grads, (((0,), (0,)), ((), ())), preferred_ele...  4.88 us
    unnamed x17, local copies, waits for them, and re-layouts  4.38 us
  transfers between devices with their start and end apart: 3, of which 3 were waited for; matrix products, arithmetic and copies ran while one was open for 3% of the time, Pallas kernels for 0%

commit v1 on v0

v1 whole, which is shorter than its diff:
```python
import jax
import jax.numpy as jnp
from jax import lax
from jax.experimental import pallas as pl
from jax.experimental.pallas import tpu as pltpu
from jax.sharding import PartitionSpec as P

MESH = pl.DeviceIdType.MESH
F32 = jnp.float32
BF16 = jnp.bfloat16

ROWS = 4096
HD = 128
NZ = 8
NDP = 64
NX, NY = 4, 8
REGION = 64
TOK = 128
NCH = 8
CW = ROWS // NCH
NBINS = 16

beta_first = 0.9
beta_second = 0.95
learn_rate = 0.001
decay_rate = 0.1
epsilon = 1e-06
adam_epsilon = 1e-08
step_count = 10.0

NEAR_FIRST = (0, 1, 7, 2, 6, 3, 5, 4)


def dot(a, b):
    return lax.dot_general(a, b, (((1,), (0,)), ((), ())), preferred_element_type=F32)


def dot_t(a, b):
    return lax.dot_general(a, b, (((0,), (0,)), ((), ())), preferred_element_type=F32)


def split3(v):
    high = v.astype(BF16)
    rest = v - high.astype(F32)
    mid = rest.astype(BF16)
    low = (rest - mid.astype(F32)).astype(BF16)
    return high, mid, low


def kernel(
    feat, kg, err_in, sel_ref, edges, thr, mom, sec, mas,
    keys_out, err_out, mom_out, sec_out, mas_out,
    fbuf, gbuf, ein, acc, maskb, memb, vbuf, errb, ebins, tiles, got, eng, wbuf, kacc, kout, state, news,
    lsem, isem, osem, zsend, zrecv, tsend, trecv, gsend, grecv, wsend, wa, wb, wc,
):
    z = lax.axis_index("tensor")
    me = lax.axis_index("dp")
    right, left = lax.rem(z + 1, NZ), lax.rem(z + NZ - 1, NZ)

    def load(c):
        return pltpu.make_async_copy(
            feat.at[:, pl.ds(pl.multiple_of(c * CW, CW), CW)], fbuf.at[z, c], lsem.at[c]
        )

    for c in range(NCH):
        load(c).start()
    loads = [
        pltpu.make_async_copy(kg, gbuf, isem.at[0]),
        pltpu.make_async_copy(err_in.at[0], ein, isem.at[1]),
        pltpu.make_async_copy(mom, state.at[0], isem.at[2]),
        pltpu.make_async_copy(sec, state.at[1], isem.at[3]),
        pltpu.make_async_copy(mas, state.at[2], isem.at[4]),
    ]
    for copy in loads:
        copy.start()

    barrier = pltpu.get_barrier_semaphore()
    for near in (left, right):
        pl.semaphore_signal(barrier, inc=1, device_id={"tensor": near}, device_id_type=MESH)

    def greet(k, carry):
        pl.semaphore_signal(
            barrier, inc=1, device_id={"dp": lax.rem(me + k, NDP)}, device_id_type=MESH
        )
        return carry

    lax.fori_loop(1, NDP, greet, 0)
    pl.semaphore_wait(barrier, NDP + 1)

    def hop(way, h, c, origin):
        return pltpu.make_async_remote_copy(
            src_ref=fbuf.at[origin, c],
            dst_ref=fbuf.at[origin, c],
            send_sem=zsend.at[way, 0 if h < 4 else 1],
            recv_sem=zrecv.at[way, h - 1, c],
            device_id={"tensor": right if way == 0 else left},
            device_id_type=MESH,
        )

    def first(c, carry):
        load(c).wait()
        hop(0, 1, c, z).start()
        hop(1, 1, c, z).start()
        return carry

    lax.fori_loop(0, NCH, first, 0)

    sel = sel_ref[0]
    sub = lax.broadcasted_iota(jnp.int32, (HD, HD), 0)
    lane = lax.broadcasted_iota(jnp.int32, (HD, HD), 1)
    group_hot = jnp.where(sub[:32] == lax.shift_right_logical(sel, 7), 1.0, 0.0).astype(BF16)
    place_hot = jnp.where(sub == lax.bitwise_and(sel, 127), 1.0, 0.0).astype(BF16)
    chosen = lax.dot_general(
        group_hot, place_hot, (((1,), (1,)), ((), ())), preferred_element_type=F32
    )
    same = lax.shift_right_logical(sub, 6) == lax.shift_right_logical(lane, 6)
    before = jnp.where(same & (sub < lane), 1.0, 0.0).astype(BF16)
    rank = dot(chosen.astype(BF16), before)
    half = lax.shift_right_logical(lane[:32], 6).astype(F32) * 8.0
    slots = jnp.where(chosen > 0.5, half + rank, -1.0)
    for g in range(32):
        vbuf[g] = slots[g : g + 1]

    bin_of = lax.broadcasted_iota(jnp.int32, (NBINS, CW), 0)
    low_edge = jnp.zeros((NBINS, CW), jnp.int32)
    high_edge = jnp.zeros((NBINS, CW), jnp.int32)
    for b in range(NBINS):
        low_edge = jnp.where(bin_of == b, edges[b], low_edge)
        high_edge = jnp.where(bin_of == b, edges[b + 1], high_edge)
    row_of = lax.broadcasted_iota(jnp.int32, (NBINS, CW), 1)
    ones = jnp.ones((HD, HD), BF16)
    row_col = lax.broadcasted_iota(jnp.int32, (CW, HD), 0)

    for copy in loads[:2]:
        copy.wait()

    def shard_of(origin):
        return gbuf[pl.ds(pl.multiple_of(origin * TOK, TOK), TOK), :]

    def prepare(c, carry):
        rows = row_of + c * CW
        memb[c] = jnp.where((rows >= low_edge) & (rows < high_edge), 1.0, 0.0).astype(BF16)
        hit = jnp.where(row_col + c * CW == sel, 1.0, 0.0).astype(BF16)
        maskb[c] = dot(hit, ones)
        acc[c] = ein[pl.ds(pl.multiple_of(c * CW, CW), CW), :].astype(F32) + dot_t(
            fbuf[z, c], shard_of(z)
        )
        return carry

    lax.fori_loop(0, NCH, prepare, 0)
    ebins[...] = jnp.zeros_like(ebins)

    for h in (1, 2, 3):
        low = lax.rem(z + NZ - h, NZ)
        high = lax.rem(z + h, NZ)

        def step(c, carry, h=h, low=low, high=high):
            hop(0, h, c, low).wait_recv()
            if h < 3:
                hop(0, h + 1, c, low).start()
            else:

                @pl.when(c < NCH // 2)
                def _():
                    hop(0, 4, c, low).start()

            hop(1, h, c, high).wait_recv()
            if h < 3:
                hop(1, h + 1, c, high).start()
            else:

                @pl.when(c >= NCH // 2)
                def _():
                    hop(1, 4, c, high).start()

            acc[c] = acc[c] + (
                dot_t(fbuf[low, c], shard_of(low)) + dot_t(fbuf[high, c], shard_of(high))
            )
            return carry

        lax.fori_loop(0, NCH, step, 0)

    far = lax.rem(z + NZ // 2, NZ)
    sub16 = lax.broadcasted_iota(jnp.int32, (16, HD), 0)
    slot16 = sub16.astype(F32)
    map_line = lax.rem(sub16, 8) == 6

    def block_copy(owner):
        return pltpu.make_async_remote_copy(
            src_ref=tiles.at[owner],
            dst_ref=got.at[me],
            send_sem=tsend,
            recv_sem=trecv,
            device_id={"dp": owner},
            device_id_type=MESH,
        )

    def err_copy(c):
        return pltpu.make_async_copy(
            errb.at[c], err_out.at[0, pl.ds(pl.multiple_of(c * CW, CW), CW), :], osem.at[c]
        )

    def finish(c):
        total = acc[c] + dot_t(fbuf[far, c], shard_of(far))
        errb[c] = jnp.where(maskb[c] > 0.5, 0.0, total).astype(BF16)
        err_copy(c).start()
        square = total * total
        top = square.astype(BF16)
        rest = (square - top.astype(F32)).astype(BF16)
        ebins[...] += dot(memb[c], top) + dot(memb[c], rest)
        parts = split3(total)
        for g in range(4):
            line = vbuf[c * 4 + g]
            pick = jnp.where(slot16 == line, 1.0, 0.0).astype(BF16)
            picked = [dot(pick, part[g * HD : (g + 1) * HD]) for part in parts]
            tile = jnp.where(map_line, line, (picked[0] + picked[1]) + picked[2])
            tiles[pl.ds(c * 8 + 2 * g, 2)] = tile.reshape(2, 8, HD)
        for j in range(8):
            owner = c * 8 + j

            @pl.when(owner != me)
            def _():
                block_copy(owner).start()

            @pl.when(owner == me)
            def _():
                got[me] = tiles[owner]

    def last(i, carry):
        for way in (0, 1):
            c = i + way * (NCH // 2)
            hop(way, 4, c, far).wait_recv()
            finish(c)
        return carry

    lax.fori_loop(0, NCH // 2, last, 0)

    lane16 = lax.broadcasted_iota(jnp.int32, (NBINS, HD), 1)
    bin_sum = jnp.sum(ebins[...], axis=1, keepdims=True)
    eng[me] = jnp.sum(jnp.where(lane16 == sub16, bin_sum, 0.0), axis=0, keepdims=True)

    def energy_copy(k):
        return pltpu.make_async_remote_copy(
            src_ref=eng.at[me],
            dst_ref=eng.at[me],
            send_sem=gsend,
            recv_sem=grecv,
            device_id={"dp": lax.rem(me + k, NDP)},
            device_id_type=MESH,
        )

    def tell(k, carry):
        energy_copy(k).start()
        return carry

    lax.fori_loop(1, NDP, tell, 0)

    for copy in loads[2:]:
        copy.wait()
    others = NDP - 1
    pltpu.make_async_copy(got.at[pl.ds(0, others)], got.at[pl.ds(0, others)], trecv).wait()
    parity = lax.rem(me, 2)
    block = got[...]
    want = (lax.broadcasted_iota(jnp.int32, (NDP, 8, HD), 1) + 8 * parity).astype(F32)
    hot = jnp.where(want == block[:, 6:7, :], 1.0, 0.0).astype(BF16).reshape(NDP * 8, HD)
    parts = split3(block.reshape(NDP * 8, HD))
    both = (dot_t(hot, parts[0]) + dot_t(hot, parts[1])) + dot_t(hot, parts[2])
    kept_sum = both[:REGION] + both[REGION:]

    lane1 = lax.broadcasted_iota(jnp.int32, (1, HD), 1)
    low1 = jnp.zeros((1, HD), jnp.int32)
    high1 = jnp.zeros((1, HD), jnp.int32)
    for b in range(NBINS):
        low1 = jnp.where(lane1 == b, edges[b], low1)
        high1 = jnp.where(lane1 == b, edges[b + 1], high1)
    width = jnp.where(lane1 < NBINS, high1 - low1, 1).astype(F32)
    own_row = me * REGION + lax.broadcasted_iota(jnp.int32, (REGION, HD), 0)
    in_bin = (own_row >= low1) & (own_row < high1)

    pltpu.make_async_copy(eng.at[pl.ds(0, others)], eng.at[pl.ds(0, others)], grecv).wait()
    energy = jnp.sum(eng[...], axis=0)
    normal = 1.0 / jnp.sqrt(energy / (float(NDP * HD) * width) + epsilon)
    scale = jnp.where(lane1 >= thr[0], normal, 1.0)
    row_scale = jnp.sum(jnp.where(in_bin, scale, 0.0), axis=1, keepdims=True)
    grad = kept_sum * row_scale
    moment_new = beta_first * state[0] + (1.0 - beta_first) * grad
    second_new = beta_second * state[1] + (1.0 - beta_second) * grad * grad
    first_hat = moment_new / (1.0 - beta_first**step_count)
    second_hat = second_new / (1.0 - beta_second**step_count)
    master = state[2]
    master_new = master - learn_rate * (
        first_hat / (jnp.sqrt(second_hat) + adam_epsilon) + decay_rate * master
    )
    wbuf[me] = master_new.astype(BF16)
    news[0] = moment_new
    news[1] = second_new
    news[2] = master_new

    x, y, core = me // (2 * NY), lax.rem(me // 2, NY), lax.rem(me, 2)
    partner = me + 1 - 2 * core

    def device(dx, dy, c):
        return (lax.rem(x + dx, NX) * NY + lax.rem(y + dy, NY)) * 2 + c

    def weight_copy(slot, to, sem):
        return pltpu.make_async_remote_copy(
            src_ref=wbuf.at[slot],
            dst_ref=wbuf.at[slot],
            send_sem=wsend,
            recv_sem=sem,
            device_id={"dp": to},
            device_id_type=MESH,
        )

    for k in NEAR_FIRST[1:]:
        weight_copy(me, device(0, k, core), wa.at[k]).start()
    outs = [
        pltpu.make_async_copy(news.at[0], mom_out, isem.at[5]),
        pltpu.make_async_copy(news.at[1], sec_out, isem.at[6]),
        pltpu.make_async_copy(news.at[2], mas_out, isem.at[7]),
    ]
    for k in NEAR_FIRST:
        slot = device(0, NY - k, core)
        if k:
            weight_copy(slot, partner, wa.at[k]).wait_recv()
        for d in (1, 3, 2):
            weight_copy(slot, device(d, 0, core), wb.at[d - 1, k]).start()
        weight_copy(slot, partner, wc.at[0, k]).start()
    for copy in outs:
        copy.start()

    kacc[...] = jnp.zeros_like(kacc)

    def project(d):
        for k in NEAR_FIRST:
            weight_copy(device(NX - d, NY - k, 1 - core), partner, wc.at[d, k]).wait_recv()
        where_x = lax.rem(x + NX - d, NX)
        for part in range(2):
            c = where_x * 2 + part
            weight = wbuf[pl.ds(c * 8, 8)].reshape(CW, HD)
            kacc[...] += dot(fbuf[:, c].reshape(NZ * TOK, CW), weight)

    done = 0
    for d in (1, 3, 2):
        for k in NEAR_FIRST:
            slot = device(NX - d, NY - k, core)
            weight_copy(slot, partner, wb.at[d - 1, k]).wait_recv()
            weight_copy(slot, partner, wc.at[d, k]).start()
        project(done)
        done = d
    project(done)
    kout[...] = kacc[...].astype(BF16)
    keys_copy = pltpu.make_async_copy(kout, keys_out, isem.at[0])
    keys_copy.start()

    for way in (0, 1):
        pltpu.make_async_copy(
            fbuf.at[pl.ds(0, 3)], fbuf.at[pl.ds(0, 3)], zsend.at[way, 0]
        ).wait()
        pltpu.make_async_copy(
            fbuf.at[0, pl.ds(0, 4)], fbuf.at[0, pl.ds(0, 4)], zsend.at[way, 1]
        ).wait()
    pltpu.make_async_copy(got.at[pl.ds(0, others)], got.at[pl.ds(0, others)], tsend).wait()
    pltpu.make_async_copy(eng.at[pl.ds(0, others)], eng.at[pl.ds(0, others)], gsend).wait()
    pltpu.make_async_copy(wbuf.at[pl.ds(0, others)], wbuf.at[pl.ds(0, others)], wsend).wait()
    for c in range(NCH):
        err_copy(c).wait()
    for copy in outs:
        copy.wait()
    keys_copy.wait()


def shards(features, key_grads, error_in, selected, bin_edges, threshold, moment, second, master):
    anywhere = pl.BlockSpec(memory_space=pl.ANY)
    vmem = pl.BlockSpec(memory_space=pltpu.VMEM)
    smem = pl.BlockSpec(memory_space=pltpu.SMEM)
    dma = pltpu.SemaphoreType.DMA
    state_shape = jax.ShapeDtypeStruct((REGION, HD), F32)
    return pl.pallas_call(
        kernel,
        out_shape=(
            jax.ShapeDtypeStruct((NZ * TOK, HD), BF16),
            jax.ShapeDtypeStruct((1, ROWS, HD), BF16),
            state_shape,
            state_shape,
            state_shape,
        ),
        in_specs=[anywhere, anywhere, anywhere, vmem, smem, smem, anywhere, anywhere, anywhere],
        out_specs=(anywhere,) * 5,
        scratch_shapes=[
            pltpu.VMEM((NZ, NCH, TOK, CW), BF16),
            pltpu.VMEM((NZ * TOK, HD), BF16),
            pltpu.VMEM((ROWS, HD), BF16),
            pltpu.VMEM((NCH, CW, HD), F32),
            pltpu.VMEM((NCH, CW, HD), F32),
            pltpu.VMEM((NCH, NBINS, CW), BF16),
            pltpu.VMEM((32, 1, HD), F32),
            pltpu.VMEM((NCH, CW, HD), BF16),
            pltpu.VMEM((NBINS, HD), F32),
            pltpu.VMEM((NDP, 8, HD), F32),
            pltpu.VMEM((NDP, 8, HD), F32),
            pltpu.VMEM((NDP, 1, HD), F32),
            pltpu.VMEM((NDP, REGION, HD), BF16),
            pltpu.VMEM((NZ * TOK, HD), F32),
            pltpu.VMEM((NZ * TOK, HD), BF16),
            pltpu.VMEM((3, REGION, HD), F32),
            pltpu.VMEM((3, REGION, HD), F32),
            dma((NCH,)),
            dma((8,)),
            dma((NCH,)),
            dma((2, 2)),
            dma((2, 4, NCH)),
            dma,
            dma,
            dma,
            dma,
            dma,
            dma((NY,)),
            dma((NX - 1, NY)),
            dma((NX, NY)),
        ],
        compiler_params=pltpu.CompilerParams(
            collective_id=0, has_side_effects=True, vmem_limit_bytes=48 * 1024 * 1024
        ),
        name="step",
    )(features, key_grads, error_in, selected, bin_edges, threshold, moment, second, master)


def solution(mesh):
    in_specs = (
        P(("dp", "tensor"), None),
        P("dp", "tensor"),
        P("dp", None, "tensor"),
        P("dp", "tensor", None),
        P(),
        P(),
        P("dp", "tensor"),
        P("dp", "tensor"),
        P("dp", "tensor"),
    )
    out_specs = (
        P("dp", "tensor"),
        P("dp", None, "tensor"),
        P("dp", "tensor"),
        P("dp", "tensor"),
        P("dp", "tensor"),
    )
    return jax.shard_map(shards, mesh=mesh, in_specs=in_specs, out_specs=out_specs, check_vma=False)
```

time: 217 us -> 136 us (0.63)
  waiting for transfers between devices: 137 us -> 0 us
  Pallas kernels: 0 us -> 125 us
  starting transfers between devices: 16.8 us -> 0 us
  blocking collectives: 15.6 us -> 0 us
  between operations: 14.9 us -> 1.35 us
  matrix products: 12.8 us -> 0 us
  local copies, waits for them, and re-layouts: 14.9 us -> 9.19 us
  other arithmetic: 4.47 us -> 0 us
    pallas_call x0 -> x1, Pallas kernels: none -> 125 us  [shards(): pl.pallas_call(kernel, out_shape=(jax.ShapeDtypeStruct((NZ * TOK, HD), BF...]
    all_gather x1 -> x0, waiting for transfers between devices: 103 us -> none  [shards(): whole = lax.all_gather(features, 'tensor', axis=0, tiled=True)]
    all_to_all x2 -> x0, waiting for transfers between devices: 32.9 us -> none  [copy_for_each(): lax.all_to_all(jnp.broadcast_to(value[None], (devices, *value.shape)), ax...]
    all_to_all x2 -> x0, starting transfers between devices: 16.7 us -> none  [copy_for_each(): lax.all_to_all(jnp.broadcast_to(value[None], (devices, *value.shape)), ax...]
    all_to_all x1 -> x0, blocking collectives: 15.6 us -> none  [in_one_piece(): lax.all_to_all(both, axis, split_axis=split_dim, concat_axis=concat_dim,...]
    dot_general x5 -> x0, matrix products: 12.8 us -> none  [the longest x1 6.29 us: shards(): jnp.dot(whole, gather_directly(weight, 'dp', 0), preferred_element_type=j...]
    unnamed x17 -> x21, local copies, waits for them, and re-layouts: 4.38 us -> 9.19 us
    scatter x3 -> x0, local copies, waits for them, and re-layouts: 3.87 us -> none  [the longest x1 1.9 us: shards(): jnp.zeros((owners * CAP, width_head), jnp.float32).at[slot]]
  transfers between devices with their start and end apart: 3 -> 0, of which waited for: 3 -> 0; matrix products, arithmetic and copies ran while one was open for 3% -> 0% of each run, Pallas kernels for 0% -> 0%
where the time goes in v1:
time: 136 us
  Pallas kernels  125 us (92%)
  local copies, waits for them, and re-layouts  9.19 us (7%)
    pallas_call x1, Pallas kernels, shards(): pl.pallas_call(kernel, out_shape=(jax.ShapeDtypeStruct((NZ * TOK, HD), BF...  125 us
    unnamed x21, local copies, waits for them, and re-layouts  9.19 us

profile of v1, /device:TPU:1, one launch (start us, length us, event | category | flops | bytes accessed | tf_op | source)
XLA Modules:
  0.0 135.6 jit_solution(17497478440153330935)
XLA Ops:
  0.6 0.0 copy-start.7
  0.6 0.0 copy-start.6
  1.3 0.0 copy-done.7
  1.3 0.0 copy-done.6
  1.3 0.0 copy-start
  1.3 1.2 copy-done
  2.6 0.0 copy-start.1
  2.6 1.2 copy-done.1
  3.8 0.0 copy-start.2
  3.8 0.9 copy-done.2
  4.7 0.0 copy-start.3
  4.7 0.8 copy-done.3
  5.5 0.0 copy-start.4
  5.5 0.8 copy-done.4
  6.3 0.0 copy-start.5
  6.3 0.8 copy-done.5
  7.0 125.1 %step.1 = (bf16[1024,128]{1,0:T(8,128)(2,1)S(1)}, bf16[1,4096,128]{2,1,0:T(8,128)(2,1)S(1)}, f32[64,128]{1,0:T(8,128)S(1)}, f32[64,128]{1,0:T(8,128)S(1)}, f32[64,128]{1,0:T(8,128)S(1)}) custom-call(bf16[128,4096]{1,0:T(8,128)(2,1)S(1)} %copy-done, bf16[1024,128]{1,0:T(8,128)(2,1)S(1)} %copy-done.2, bf16[1,4096,128]{2,1,0:T(8,128)(2,1)S(1)} %copy-done.1, ...), custom_call_target="tpu_custom_call" | custom-call | tf_op jit(solution)/shard_map/step/pallas_call | solution.py:379
  132.1 0.7 copy.20
  132.8 1.0 copy.21
  133.8 0.6 copy.22
  134.4 0.6 copy.23
  135.0 0.6 copy.24
Async XLA Ops:
  0.6 0.7 copy-start.7
  0.6 0.7 copy-start.6
  1.3 1.2 copy-start
  2.6 1.2 copy-start.1
  3.8 0.9 copy-start.2
  4.7 0.8 copy-start.3
  5.5 0.8 copy-start.4
  6.3 0.8 copy-start.5

commit v2 on v1

--- a/solution.py
+++ b/solution.py
@@ -51,7 +51,7 @@
     feat, kg, err_in, sel_ref, edges, thr, mom, sec, mas,
     keys_out, err_out, mom_out, sec_out, mas_out,
     fbuf, gbuf, ein, acc, maskb, memb, vbuf, errb, ebins, tiles, got, eng, wbuf, kacc, kout, state, news,
-    lsem, isem, osem, zsend, zrecv, tsend, trecv, gsend, grecv, wsend, wa, wb, wc,
+    lsem, isem, osem, meet, zsend, zrecv, tsend, trecv, gsend, grecv, wsend, wa, wb, wc,
 ):
     z = lax.axis_index("tensor")
     me = lax.axis_index("dp")
@@ -75,17 +75,19 @@
         copy.start()
 
     barrier = pltpu.get_barrier_semaphore()
+    x, y, core = me // (2 * NY), lax.rem(me // 2, NY), lax.rem(me, 2)
+    partner = me + 1 - 2 * core
+
+    def device(dx, dy, c):
+        return (lax.rem(x + dx, NX) * NY + lax.rem(y + dy, NY)) * 2 + c
+
+    along_x = (device(1, 0, core), device(NX - 1, 0, core))
+    along_y = (device(0, 1, core), device(0, NY - 1, core))
     for near in (left, right):
         pl.semaphore_signal(barrier, inc=1, device_id={"tensor": near}, device_id_type=MESH)
-
-    def greet(k, carry):
-        pl.semaphore_signal(
-            barrier, inc=1, device_id={"dp": lax.rem(me + k, NDP)}, device_id_type=MESH
-        )
-        return carry
-
-    lax.fori_loop(1, NDP, greet, 0)
-    pl.semaphore_wait(barrier, NDP + 1)
+    for near in (*along_x, *along_y, partner):
+        pl.semaphore_signal(barrier, inc=1, device_id={"dp": near}, device_id_type=MESH)
+    pl.semaphore_wait(barrier, 7)
 
     def hop(way, h, c, origin):
         return pltpu.make_async_remote_copy(
@@ -104,6 +106,11 @@
         return carry
 
     lax.fori_loop(0, NCH, first, 0)
+
+    for turn, nears in enumerate((along_y, along_y, along_y, along_x, along_x, (partner,))):
+        for near in nears:
+            pl.semaphore_signal(meet.at[turn], inc=1, device_id={"dp": near}, device_id_type=MESH)
+        pl.semaphore_wait(meet.at[turn], len(nears))
 
     sel = sel_ref[0]
     sub = lax.broadcasted_iota(jnp.int32, (HD, HD), 0)
@@ -292,15 +299,6 @@
         first_hat / (jnp.sqrt(second_hat) + adam_epsilon) + decay_rate * master
     )
     wbuf[me] = master_new.astype(BF16)
-    news[0] = moment_new
-    news[1] = second_new
-    news[2] = master_new
-
-    x, y, core = me // (2 * NY), lax.rem(me // 2, NY), lax.rem(me, 2)
-    partner = me + 1 - 2 * core
-
-    def device(dx, dy, c):
-        return (lax.rem(x + dx, NX) * NY + lax.rem(y + dy, NY)) * 2 + c
 
     def weight_copy(slot, to, sem):
         return pltpu.make_async_remote_copy(
@@ -314,6 +312,9 @@
 
     for k in NEAR_FIRST[1:]:
         weight_copy(me, device(0, k, core), wa.at[k]).start()
+    news[0] = moment_new
+    news[1] = second_new
+    news[2] = master_new
     outs = [
         pltpu.make_async_copy(news.at[0], mom_out, isem.at[5]),
         pltpu.make_async_copy(news.at[1], sec_out, isem.at[6]),
@@ -370,23 +371,47 @@
     keys_copy.wait()
 
 
+def put_out(
+    keys, err, mom, sec, mas, keys_to, err_to, mom_to, sec_to, mas_to,
+    keys_at, err_at, state_at, arrive, leave,
+):
+    quarter = ROWS // 4
+    routes = []
+    for q in range(4):
+        rows = pl.ds(q * quarter, quarter)
+        routes.append((err.at[0, rows, :], err_at.at[rows, :], err_to.at[0, rows, :]))
+    routes.append((keys, keys_at, keys_to))
+    for k, (a, b) in enumerate(((mom, mom_to), (sec, sec_to), (mas, mas_to))):
+        routes.append((a, state_at.at[k], b))
+    first = [pltpu.make_async_copy(a, b, arrive.at[k]) for k, (a, b, _) in enumerate(routes)]
+    second = [pltpu.make_async_copy(b, c, leave.at[k]) for k, (_, b, c) in enumerate(routes)]
+    for copy in first:
+        copy.start()
+    for one, two in zip(first, second):
+        one.wait()
+        two.start()
+    for copy in second:
+        copy.wait()
+
+
 def shards(features, key_grads, error_in, selected, bin_edges, threshold, moment, second, master):
-    anywhere = pl.BlockSpec(memory_space=pl.ANY)
+    hbm = pl.BlockSpec(memory_space=pltpu.HBM)
     vmem = pl.BlockSpec(memory_space=pltpu.VMEM)
     smem = pl.BlockSpec(memory_space=pltpu.SMEM)
     dma = pltpu.SemaphoreType.DMA
     state_shape = jax.ShapeDtypeStruct((REGION, HD), F32)
-    return pl.pallas_call(
+    out_shape = (
+        jax.ShapeDtypeStruct((NZ * TOK, HD), BF16),
+        jax.ShapeDtypeStruct((1, ROWS, HD), BF16),
+        state_shape,
+        state_shape,
+        state_shape,
+    )
+    results = pl.pallas_call(
         kernel,
-        out_shape=(
-            jax.ShapeDtypeStruct((NZ * TOK, HD), BF16),
-            jax.ShapeDtypeStruct((1, ROWS, HD), BF16),
-            state_shape,
-            state_shape,
-            state_shape,
-        ),
-        in_specs=[anywhere, anywhere, anywhere, vmem, smem, smem, anywhere, anywhere, anywhere],
-        out_specs=(anywhere,) * 5,
+        out_shape=out_shape,
+        in_specs=[hbm, hbm, hbm, vmem, smem, smem, hbm, hbm, hbm],
+        out_specs=(hbm,) * 5,
         scratch_shapes=[
             pltpu.VMEM((NZ, NCH, TOK, CW), BF16),
             pltpu.VMEM((NZ * TOK, HD), BF16),
@@ -408,6 +433,7 @@
             dma((NCH,)),
             dma((8,)),
             dma((NCH,)),
+            pltpu.SemaphoreType.REGULAR((6,)),
             dma((2, 2)),
             dma((2, 4, NCH)),
             dma,
@@ -420,10 +446,25 @@
             dma((NX, NY)),
         ],
         compiler_params=pltpu.CompilerParams(
-            collective_id=0, has_side_effects=True, vmem_limit_bytes=48 * 1024 * 1024
+            collective_id=0, has_side_effects=True, vmem_limit_bytes=58 * 1024 * 1024
         ),
         name="step",
     )(features, key_grads, error_in, selected, bin_edges, threshold, moment, second, master)
+    return pl.pallas_call(
+        put_out,
+        out_shape=out_shape,
+        in_specs=[hbm] * 5,
+        out_specs=(hbm,) * 5,
+        scratch_shapes=[
+            pltpu.VMEM((NZ * TOK, HD), BF16),
+            pltpu.VMEM((ROWS, HD), BF16),
+            pltpu.VMEM((3, REGION, HD), F32),
+            dma((8,)),
+            dma((8,)),
+        ],
+        compiler_params=pltpu.CompilerParams(vmem_limit_bytes=58 * 1024 * 1024),
+        name="put_out",
+    )(*results)
 
 
 def solution(mesh):

time: 136 us -> 125 us (0.919)
  local copies, waits for them, and re-layouts: 9.19 us -> 0 us
  Pallas kernels: 125 us -> 123 us
    unnamed x21 -> x0, local copies, waits for them, and re-layouts: 9.19 us -> none
    pallas_call x1 -> x2, Pallas kernels: 125 us -> 123 us  [the longest x1 121 us: shards(): pl.pallas_call(kernel, out_shape=out_shape, in_specs=[hbm, hbm, hbm, vmem...]
where the time goes in v2:
time: 125 us; the launch traced here: 124 us
  Pallas kernels  123 us (98%)
  between operations  1.29 us (1%)
    pallas_call x1, Pallas kernels, shards(): pl.pallas_call(kernel, out_shape=out_shape, in_specs=[hbm, hbm, hbm, vmem...  121 us

profile of v2, /device:TPU:1, one launch (start us, length us, event | category | flops | bytes accessed | tf_op | source)
XLA Modules:
  0.0 124.4 jit_solution(5544639862939243165)
XLA Ops:
  1.3 120.9 %step.1 = (bf16[1024,128]{1,0:T(8,128)(2,1)}, bf16[1,4096,128]{2,1,0:T(8,128)(2,1)}, f32[64,128]{1,0:T(8,128)}, f32[64,128]{1,0:T(8,128)}, f32[64,128]{1,0:T(8,128)}) custom-call(bf16[128,4096]{1,0:T(8,128)(2,1)} %feat.1, bf16[1024,128]{1,0:T(8,128)(2,1)} %kg.1, bf16[1,4096,128]{2,1,0:T(8,128)(2,1)} %err_in.1, s32[1,1,128]{2,1,0:T(1,128)} %sel_ref.1, ...), custom_call_target="tpu_custom_call" | custom-call | tf_op jit(solution)/shard_map/step/pallas_call | solution.py:410
  122.2 2.2 %put_out.1 = (bf16[1024,128]{1,0:T(8,128)(2,1)}, bf16[1,4096,128]{2,1,0:T(8,128)(2,1)}, f32[64,128]{1,0:T(8,128)}, f32[64,128]{1,0:T(8,128)}, f32[64,128]{1,0:T(8,128)}) custom-call(bf16[1024,128]{1,0:T(8,128)(2,1)} %get-tuple-element.10.keys, bf16[1,4096,128]{2,1,0:T(8,128)(2,1)} %get-tuple-element.11.err, f32[64,128]{1,0:T(8,128)} %get-tuple-element.12.mom, ...), custom_call_target="tpu_custom_call" | custom-call | tf_op jit(solution)/shard_map/put_out/pallas_call | solution.py:453

commit v3 on v2

--- a/solution.py
+++ b/solution.py
@@ -16,8 +16,10 @@
 NX, NY = 4, 8
 REGION = 64
 TOK = 128
-NCH = 8
+NCH = 16
+HALF = NCH // 2
 CW = ROWS // NCH
+OWNERS = CW // REGION
 NBINS = 16
 
 beta_first = 0.9
@@ -29,6 +31,8 @@
 step_count = 10.0
 
 NEAR_FIRST = (0, 1, 7, 2, 6, 3, 5, 4)
+FAR_FIRST_Y = (4, 3, 5, 2, 6, 1, 7, 0)
+FAR_FIRST_X = (2, 1, 3, 0)
 
 
 def dot(a, b):
@@ -57,13 +61,58 @@
     me = lax.axis_index("dp")
     right, left = lax.rem(z + 1, NZ), lax.rem(z + NZ - 1, NZ)
 
+    barrier = pltpu.get_barrier_semaphore()
+    x, y, core = me // (2 * NY), lax.rem(me // 2, NY), lax.rem(me, 2)
+    partner = me + 1 - 2 * core
+
+    at_x = [lax.rem(x + d, NX) * (2 * NY) for d in range(NX)]
+    at_y = [lax.rem(y + d, NY) * 2 for d in range(NY)]
+
+    def device(dx, dy, c):
+        return at_x[dx % NX] + at_y[dy % NY] + c
+
+    along_x = (device(1, 0, core), device(NX - 1, 0, core))
+    along_y = (device(0, 1, core), device(0, NY - 1, core))
+    for near in (left, right):
+        pl.semaphore_signal(barrier, inc=1, device_id={"tensor": near}, device_id_type=MESH)
+    for near in (*along_x, *along_y, partner):
+        pl.semaphore_signal(barrier, inc=1, device_id={"dp": near}, device_id_type=MESH)
+
     def load(c):
         return pltpu.make_async_copy(
             feat.at[:, pl.ds(pl.multiple_of(c * CW, CW), CW)], fbuf.at[z, c], lsem.at[c]
         )
 
-    for c in range(NCH):
-        load(c).start()
+    pl.semaphore_wait(barrier, 7)
+
+    def hop(way, h, c, origin):
+        return pltpu.make_async_remote_copy(
+            src_ref=fbuf.at[origin, c],
+            dst_ref=fbuf.at[origin, c],
+            send_sem=zsend.at[way, 0 if h < 4 else 1],
+            recv_sem=zrecv.at[way, h - 1, c],
+            device_id={"tensor": right if way == 0 else left},
+            device_id_type=MESH,
+        )
+
+    def first(i, carry):
+        for way in (0, 1):
+            c = lax.rem(i + way * HALF, NCH)
+            pltpu.make_async_remote_copy(
+                src_ref=feat.at[:, pl.ds(pl.multiple_of(c * CW, CW), CW)],
+                dst_ref=fbuf.at[z, c],
+                send_sem=zsend.at[way, 0],
+                recv_sem=zrecv.at[way, 0, c],
+                device_id={"tensor": right if way == 0 else left},
+                device_id_type=MESH,
+            ).start()
+        return carry
+
+    lax.fori_loop(0, NCH, first, 0)
+
+    for i in range(HALF):
+        load(i).start()
+        load(i + HALF).start()
     loads = [
         pltpu.make_async_copy(kg, gbuf, isem.at[0]),
         pltpu.make_async_copy(err_in.at[0], ein, isem.at[1]),
@@ -73,39 +122,6 @@
     ]
     for copy in loads:
         copy.start()
-
-    barrier = pltpu.get_barrier_semaphore()
-    x, y, core = me // (2 * NY), lax.rem(me // 2, NY), lax.rem(me, 2)
-    partner = me + 1 - 2 * core
-
-    def device(dx, dy, c):
-        return (lax.rem(x + dx, NX) * NY + lax.rem(y + dy, NY)) * 2 + c
-
-    along_x = (device(1, 0, core), device(NX - 1, 0, core))
-    along_y = (device(0, 1, core), device(0, NY - 1, core))
-    for near in (left, right):
-        pl.semaphore_signal(barrier, inc=1, device_id={"tensor": near}, device_id_type=MESH)
-    for near in (*along_x, *along_y, partner):
-        pl.semaphore_signal(barrier, inc=1, device_id={"dp": near}, device_id_type=MESH)
-    pl.semaphore_wait(barrier, 7)
-
-    def hop(way, h, c, origin):
-        return pltpu.make_async_remote_copy(
-            src_ref=fbuf.at[origin, c],
-            dst_ref=fbuf.at[origin, c],
-            send_sem=zsend.at[way, 0 if h < 4 else 1],
-            recv_sem=zrecv.at[way, h - 1, c],
-            device_id={"tensor": right if way == 0 else left},
-            device_id_type=MESH,
-        )
-
-    def first(c, carry):
-        load(c).wait()
-        hop(0, 1, c, z).start()
-        hop(1, 1, c, z).start()
-        return carry
-
-    lax.fori_loop(0, NCH, first, 0)
 
     for turn, nears in enumerate((along_y, along_y, along_y, along_x, along_x, (partner,))):
         for near in nears:
@@ -145,6 +161,7 @@
         return gbuf[pl.ds(pl.multiple_of(origin * TOK, TOK), TOK), :]
 
     def prepare(c, carry):
+        load(c).wait()
         rows = row_of + c * CW
         memb[c] = jnp.where((rows >= low_edge) & (rows < high_edge), 1.0, 0.0).astype(BF16)
         hit = jnp.where(row_col + c * CW == sel, 1.0, 0.0).astype(BF16)
@@ -157,35 +174,46 @@
     lax.fori_loop(0, NCH, prepare, 0)
     ebins[...] = jnp.zeros_like(ebins)
 
-    for h in (1, 2, 3):
-        low = lax.rem(z + NZ - h, NZ)
-        high = lax.rem(z + h, NZ)
-
-        def step(c, carry, h=h, low=low, high=high):
-            hop(0, h, c, low).wait_recv()
-            if h < 3:
-                hop(0, h + 1, c, low).start()
-            else:
-
-                @pl.when(c < NCH // 2)
-                def _():
-                    hop(0, 4, c, low).start()
-
-            hop(1, h, c, high).wait_recv()
-            if h < 3:
-                hop(1, h + 1, c, high).start()
-            else:
-
-                @pl.when(c >= NCH // 2)
-                def _():
-                    hop(1, 4, c, high).start()
-
-            acc[c] = acc[c] + (
-                dot_t(fbuf[low, c], shard_of(low)) + dot_t(fbuf[high, c], shard_of(high))
-            )
-            return carry
-
-        lax.fori_loop(0, NCH, step, 0)
+    lows = [lax.rem(z + NZ - h, NZ) for h in range(4)]
+    highs = [lax.rem(z + h, NZ) for h in range(4)]
+
+    def places(i):
+        return (i, lax.rem(i + HALF, NCH))
+
+    def take(h, i):
+        for way, origin in ((0, lows[h]), (1, highs[h])):
+            c = places(i)[way]
+            acc[c] = acc[c] + dot_t(fbuf[origin, c], shard_of(origin))
+
+    def step1(i, carry):
+        for way, origin in ((0, lows[1]), (1, highs[1])):
+            hop(way, 1, places(i)[way], origin).wait_recv()
+            hop(way, 2, places(i)[way], origin).start()
+        take(1, i)
+        return carry
+
+    def step2(i, carry):
+        for way, origin in ((0, lows[2]), (1, highs[2])):
+            hop(way, 2, places(i)[way], origin).wait_recv()
+
+            @pl.when(i < HALF)
+            def _():
+                hop(way, 3, places(i)[way], origin).start()
+
+        take(2, i)
+        return carry
+
+    def step3(i, carry):
+        for way in (0, 1):
+            hop(way, 3, places(i)[way], (lows[3], highs[3])[way]).wait_recv()
+            hop(way, 3, places(i + HALF)[way], (lows[2], highs[2])[way]).start()
+            hop(way, 4, places(i)[way], (lows[3], highs[3])[way]).start()
+        take(3, i)
+        return carry
+
+    lax.fori_loop(0, NCH, step1, 0)
+    lax.fori_loop(0, NCH, step2, 0)
+    lax.fori_loop(0, HALF, step3, 0)
 
     far = lax.rem(z + NZ // 2, NZ)
     sub16 = lax.broadcasted_iota(jnp.int32, (16, HD), 0)
@@ -209,21 +237,20 @@
 
     def finish(c):
         total = acc[c] + dot_t(fbuf[far, c], shard_of(far))
-        errb[c] = jnp.where(maskb[c] > 0.5, 0.0, total).astype(BF16)
-        err_copy(c).start()
+        acc[c] = total
         square = total * total
         top = square.astype(BF16)
         rest = (square - top.astype(F32)).astype(BF16)
         ebins[...] += dot(memb[c], top) + dot(memb[c], rest)
         parts = split3(total)
-        for g in range(4):
-            line = vbuf[c * 4 + g]
+        for g in range(CW // HD):
+            line = vbuf[c * (CW // HD) + g]
             pick = jnp.where(slot16 == line, 1.0, 0.0).astype(BF16)
             picked = [dot(pick, part[g * HD : (g + 1) * HD]) for part in parts]
             tile = jnp.where(map_line, line, (picked[0] + picked[1]) + picked[2])
-            tiles[pl.ds(c * 8 + 2 * g, 2)] = tile.reshape(2, 8, HD)
-        for j in range(8):
-            owner = c * 8 + j
+            tiles[pl.ds(c * OWNERS + 2 * g, 2)] = tile.reshape(2, 8, HD)
+        for j in range(OWNERS):
+            owner = c * OWNERS + j
 
             @pl.when(owner != me)
             def _():
@@ -235,32 +262,39 @@
 
     def last(i, carry):
         for way in (0, 1):
-            c = i + way * (NCH // 2)
+            hop(way, 3, places(i + HALF)[way], (lows[3], highs[3])[way]).wait_recv()
+        take(3, i + HALF)
+        for way in (0, 1):
+            c = i + way * HALF
             hop(way, 4, c, far).wait_recv()
             finish(c)
         return carry
 
-    lax.fori_loop(0, NCH // 2, last, 0)
+    lax.fori_loop(0, HALF, last, 0)
 
     lane16 = lax.broadcasted_iota(jnp.int32, (NBINS, HD), 1)
     bin_sum = jnp.sum(ebins[...], axis=1, keepdims=True)
     eng[me] = jnp.sum(jnp.where(lane16 == sub16, bin_sum, 0.0), axis=0, keepdims=True)
 
-    def energy_copy(k):
-        return pltpu.make_async_remote_copy(
-            src_ref=eng.at[me],
-            dst_ref=eng.at[me],
-            send_sem=gsend,
-            recv_sem=grecv,
-            device_id={"dp": lax.rem(me + k, NDP)},
-            device_id_type=MESH,
-        )
-
-    def tell(k, carry):
-        energy_copy(k).start()
-        return carry
-
-    lax.fori_loop(1, NDP, tell, 0)
+    for dy in FAR_FIRST_Y:
+        for dx in FAR_FIRST_X:
+            for dc in (1, 0):
+                if dx or dy or dc:
+                    pltpu.make_async_remote_copy(
+                        src_ref=eng.at[me],
+                        dst_ref=eng.at[me],
+                        send_sem=gsend,
+                        recv_sem=grecv,
+                        device_id={"dp": device(dx, dy, 1 - core if dc else core)},
+                        device_id_type=MESH,
+                    ).start()
+
+    def residual(c, carry):
+        errb[c] = jnp.where(maskb[c] > 0.5, 0.0, acc[c]).astype(BF16)
+        err_copy(c).start()
+        return carry
+
+    lax.fori_loop(0, NCH, residual, 0)
 
     for copy in loads[2:]:
         copy.wait()
@@ -287,7 +321,7 @@
     pltpu.make_async_copy(eng.at[pl.ds(0, others)], eng.at[pl.ds(0, others)], grecv).wait()
     energy = jnp.sum(eng[...], axis=0)
     normal = 1.0 / jnp.sqrt(energy / (float(NDP * HD) * width) + epsilon)
-    scale = jnp.where(lane1 >= thr[0], normal, 1.0)
+    scale = jnp.where(lane1 >= thr[...], normal, 1.0)
     row_scale = jnp.sum(jnp.where(in_bin, scale, 0.0), axis=1, keepdims=True)
     grad = kept_sum * row_scale
     moment_new = beta_first * state[0] + (1.0 - beta_first) * grad
@@ -330,27 +364,31 @@
     for copy in outs:
         copy.start()
 
-    kacc[...] = jnp.zeros_like(kacc)
-
-    def project(d):
-        for k in NEAR_FIRST:
-            weight_copy(device(NX - d, NY - k, 1 - core), partner, wc.at[d, k]).wait_recv()
-        where_x = lax.rem(x + NX - d, NX)
-        for part in range(2):
-            c = where_x * 2 + part
-            weight = wbuf[pl.ds(c * 8, 8)].reshape(CW, HD)
-            kacc[...] += dot(fbuf[:, c].reshape(NZ * TOK, CW), weight)
-
-    done = 0
-    for d in (1, 3, 2):
+    def pass_on(d):
         for k in NEAR_FIRST:
             slot = device(NX - d, NY - k, core)
             weight_copy(slot, partner, wb.at[d - 1, k]).wait_recv()
             weight_copy(slot, partner, wc.at[d, k]).start()
-        project(done)
-        done = d
-    project(done)
-    kout[...] = kacc[...].astype(BF16)
+
+    def share(d):
+        for k in NEAR_FIRST:
+            weight_copy(device(NX - d, NY - k, 1 - core), partner, wc.at[d, k]).wait_recv()
+        where_x = lax.rem(x + NX - d, NX)
+        total = None
+        for part in range(NY // 2):
+            c = where_x * (NY // 2) + part
+            weight = wbuf[pl.ds(c * OWNERS, OWNERS)].reshape(CW, HD)
+            one = dot(fbuf[:, c].reshape(NZ * TOK, CW), weight)
+            total = one if total is None else total + one
+        return total
+
+    pass_on(1)
+    pass_on(3)
+    kacc[...] = share(0)
+    pass_on(2)
+    kacc[...] += share(1)
+    kacc[...] += share(3)
+    kout[...] = (kacc[...] + share(2)).astype(BF16)
     keys_copy = pltpu.make_async_copy(kout, keys_out, isem.at[0])
     keys_copy.start()
 
@@ -359,7 +397,7 @@
             fbuf.at[pl.ds(0, 3)], fbuf.at[pl.ds(0, 3)], zsend.at[way, 0]
         ).wait()
         pltpu.make_async_copy(
-            fbuf.at[0, pl.ds(0, 4)], fbuf.at[0, pl.ds(0, 4)], zsend.at[way, 1]
+            fbuf.at[0, pl.ds(0, HALF)], fbuf.at[0, pl.ds(0, HALF)], zsend.at[way, 1]
         ).wait()
     pltpu.make_async_copy(got.at[pl.ds(0, others)], got.at[pl.ds(0, others)], tsend).wait()
     pltpu.make_async_copy(eng.at[pl.ds(0, others)], eng.at[pl.ds(0, others)], gsend).wait()
@@ -375,10 +413,10 @@
     keys, err, mom, sec, mas, keys_to, err_to, mom_to, sec_to, mas_to,
     keys_at, err_at, state_at, arrive, leave,
 ):
-    quarter = ROWS // 4
+    eighth = ROWS // 8
     routes = []
-    for q in range(4):
-        rows = pl.ds(q * quarter, quarter)
+    for q in range(8):
+        rows = pl.ds(q * eighth, eighth)
         routes.append((err.at[0, rows, :], err_at.at[rows, :], err_to.at[0, rows, :]))
     routes.append((keys, keys_at, keys_to))
     for k, (a, b) in enumerate(((mom, mom_to), (sec, sec_to), (mas, mas_to))):
@@ -410,7 +448,7 @@
     results = pl.pallas_call(
         kernel,
         out_shape=out_shape,
-        in_specs=[hbm, hbm, hbm, vmem, smem, smem, hbm, hbm, hbm],
+        in_specs=[hbm, hbm, hbm, vmem, smem, vmem, hbm, hbm, hbm],
         out_specs=(hbm,) * 5,
         scratch_shapes=[
             pltpu.VMEM((NZ, NCH, TOK, CW), BF16),
@@ -449,7 +487,7 @@
             collective_id=0, has_side_effects=True, vmem_limit_bytes=58 * 1024 * 1024
         ),
         name="step",
-    )(features, key_grads, error_in, selected, bin_edges, threshold, moment, second, master)
+    )(features, key_grads, error_in, selected, bin_edges, threshold.reshape(1, 1), moment, second, master)
     return pl.pallas_call(
         put_out,
         out_shape=out_shape,
@@ -459,8 +497,8 @@
             pltpu.VMEM((NZ * TOK, HD), BF16),
             pltpu.VMEM((ROWS, HD), BF16),
             pltpu.VMEM((3, REGION, HD), F32),
-            dma((8,)),
-            dma((8,)),
+            dma((12,)),
+            dma((12,)),
         ],
         compiler_params=pltpu.CompilerParams(vmem_limit_bytes=58 * 1024 * 1024),
         name="put_out",

time: 125 us -> 125 us (level)
  no operation moved by 1% of the time
where the time goes in v3:
time: 125 us; the launch traced here: 124 us
  Pallas kernels  123 us (98%)
  between operations  1.29 us (1%)
    pallas_call x1, Pallas kernels, shards(): pl.pallas_call(kernel, out_shape=out_shape, in_specs=[hbm, hbm, hbm, vmem...  121 us

profile of v3, /device:TPU:1, one launch (start us, length us, event | category | flops | bytes accessed | tf_op | source)
XLA Modules:
  0.0 124.5 jit_solution(5915642019329901128)
XLA Ops:
  1.3 120.9 %step.1 = (bf16[1024,128]{1,0:T(8,128)(2,1)}, bf16[1,4096,128]{2,1,0:T(8,128)(2,1)}, f32[64,128]{1,0:T(8,128)}, f32[64,128]{1,0:T(8,128)}, f32[64,128]{1,0:T(8,128)}) custom-call(bf16[128,4096]{1,0:T(8,128)(2,1)} %feat.1, bf16[1024,128]{1,0:T(8,128)(2,1)} %kg.1, bf16[1,4096,128]{2,1,0:T(8,128)(2,1)} %err_in.1, s32[1,1,128]{2,1,0:T(1,128)} %sel_ref.1, ...), custom_call_target="tpu_custom_call" | custom-call | tf_op jit(solution)/shard_map/step/pallas_call | solution.py:448
  122.2 2.3 %put_out.1 = (bf16[1024,128]{1,0:T(8,128)(2,1)}, bf16[1,4096,128]{2,1,0:T(8,128)(2,1)}, f32[64,128]{1,0:T(8,128)}, f32[64,128]{1,0:T(8,128)}, f32[64,128]{1,0:T(8,128)}) custom-call(bf16[1024,128]{1,0:T(8,128)(2,1)} %get-tuple-element.10.keys, bf16[1,4096,128]{2,1,0:T(8,128)(2,1)} %get-tuple-element.11.err, f32[64,128]{1,0:T(8,128)} %get-tuple-element.12.mom, ...), custom_call_target="tpu_custom_call" | custom-call | tf_op jit(solution)/shard_map/put_out/pallas_call | solution.py:491

commit v4 on v3

--- a/solution.py
+++ b/solution.py
@@ -413,10 +413,10 @@
     keys, err, mom, sec, mas, keys_to, err_to, mom_to, sec_to, mas_to,
     keys_at, err_at, state_at, arrive, leave,
 ):
-    eighth = ROWS // 8
+    quarter = ROWS // 4
     routes = []
-    for q in range(8):
-        rows = pl.ds(q * eighth, eighth)
+    for q in range(4):
+        rows = pl.ds(q * quarter, quarter)
         routes.append((err.at[0, rows, :], err_at.at[rows, :], err_to.at[0, rows, :]))
     routes.append((keys, keys_at, keys_to))
     for k, (a, b) in enumerate(((mom, mom_to), (sec, sec_to), (mas, mas_to))):
@@ -497,8 +497,8 @@
             pltpu.VMEM((NZ * TOK, HD), BF16),
             pltpu.VMEM((ROWS, HD), BF16),
             pltpu.VMEM((3, REGION, HD), F32),
-            dma((12,)),
-            dma((12,)),
+            dma((8,)),
+            dma((8,)),
         ],
         compiler_params=pltpu.CompilerParams(vmem_limit_bytes=58 * 1024 * 1024),
         name="put_out",

time: 125 us -> 125 us (level)
  no operation moved by 1% of the time
where the time goes in v4:
time: 125 us; the launch traced here: 124 us
  Pallas kernels  123 us (98%)
  between operations  1.29 us (1%)
    pallas_call x1, Pallas kernels, shards(): pl.pallas_call(kernel, out_shape=out_shape, in_specs=[hbm, hbm, hbm, vmem...  121 us

profile of v4, /device:TPU:1, one launch (start us, length us, event | category | flops | bytes accessed | tf_op | source)
XLA Modules:
  0.0 124.3 jit_solution(17307267018919535053)
XLA Ops:
  1.3 120.9 %step.1 = (bf16[1024,128]{1,0:T(8,128)(2,1)}, bf16[1,4096,128]{2,1,0:T(8,128)(2,1)}, f32[64,128]{1,0:T(8,128)}, f32[64,128]{1,0:T(8,128)}, f32[64,128]{1,0:T(8,128)}) custom-call(bf16[128,4096]{1,0:T(8,128)(2,1)} %feat.1, bf16[1024,128]{1,0:T(8,128)(2,1)} %kg.1, bf16[1,4096,128]{2,1,0:T(8,128)(2,1)} %err_in.1, s32[1,1,128]{2,1,0:T(1,128)} %sel_ref.1, ...), custom_call_target="tpu_custom_call" | custom-call | tf_op jit(solution)/shard_map/step/pallas_call | solution.py:448
  122.2 2.2 %put_out.1 = (bf16[1024,128]{1,0:T(8,128)(2,1)}, bf16[1,4096,128]{2,1,0:T(8,128)(2,1)}, f32[64,128]{1,0:T(8,128)}, f32[64,128]{1,0:T(8,128)}, f32[64,128]{1,0:T(8,128)}) custom-call(bf16[1024,128]{1,0:T(8,128)(2,1)} %get-tuple-element.10.keys, bf16[1,4096,128]{2,1,0:T(8,128)(2,1)} %get-tuple-element.11.err, f32[64,128]{1,0:T(8,128)} %get-tuple-element.12.mom, ...), custom_call_target="tpu_custom_call" | custom-call | tf_op jit(solution)/shard_map/put_out/pallas_call | solution.py:491
